TPU v7x, 768 devices: a whole 4x8x12 slice. The times are simulated.
768 devices in a mesh: gx: 16 (over y, core), gy: 12 (over z), gz: 4 (over x).
Axes of the slice: x: 4, y: 8, z: 12, core: 2. Of those that a mesh axis runs over, the one named last changes fastest.
Arguments:
- right_side: float32 [16, 12, 4, 6, 128], P('gx', 'gy', 'gz')
- self_drag: float32 [16, 12, 4, 6, 128], P('gx', 'gy', 'gz'), may hold values from 0.5 to 2
- pair_tensors: float32 [16, 12, 4, 36, 256], P('gx', 'gy', 'gz')
- pair_first: int32 [16, 12, 4, 256], P('gx', 'gy', 'gz'), may hold values from 0 to 127
- pair_second: int32 [16, 12, 4, 256], P('gx', 'gy', 'gz'), may hold values from 0 to 3455
- pair_count: int32 [16, 12, 4], P('gx', 'gy', 'gz'), may hold values from 32 to 256, as said below
- particle_count: int32 [16, 12, 4], P('gx', 'gy', 'gz'), may hold values from 48 to 128, as said below
Outputs:
- solution: float32 [16, 12, 4, 6, 128], P('gx', 'gy', 'gz')
- residual: float32 [16, 12, 4, 6, 128], P('gx', 'gy', 'gz')
Inputs may be any that keep to these rules, and one draw needn't show every extreme that they name: Slots at or after pair_count of a block are unused; some block is full with 256 live pair slots in every draw. Particle slots at or after particle_count of a block are padding; some block is full in every draw. pair_second // 128 is a neighbour offset o in 0 to 26 naming the block displaced by (o//9 - 1, (o//3) mod 3 - 1, o mod 3 - 1), periodic in every dimension.
All inputs are finite; a program needn't handle non-finite values.
Results may differ from a plain program's by a relative error of at most 0.0003.
Values sent between devices are 32-bit elements; how exact they have to be, the bound alone decides.
A program may use at most 32 MiB of HBM per device.

v0:
```python
import jax
import jax.numpy as jnp
from jax import lax
from jax.sharding import PartitionSpec as P

ITERS = 2


def padded(value, sides, width):
    for axis, dim in sides:
        devices, length = (lax.axis_size(axis), value.shape[dim])
        up = [(i, (i + 1) % devices) for i in range(devices)]
        down = [(j, i) for i, j in up]
        last = lax.slice_in_dim(value, length - width, length, axis=dim)
        initial = lax.slice_in_dim(value, 0, width, axis=dim)
        before = lax.ppermute(last, axis, up)
        after = lax.ppermute(initial, axis, down)
        value = jnp.concatenate([before, value, after], axis=dim)
    return value


def component_index(block_id, slot_id, lane_count):
    component = jnp.arange(6, dtype=jnp.int32).reshape(1, 1, 1, 6, 1)
    return (block_id[:, :, :, None, :] * 6 + component) * lane_count + slot_id[:, :, :, None, :]


def tensor_apply(tensors, values):
    shaped = tensors.reshape(tensors.shape[:3] + (6, 6, tensors.shape[-1]))
    forces = shaped[:, :, :, :, 0, :] * values[:, :, :, 0:1, :]
    for column in range(1, 6):
        forces = forces + shaped[:, :, :, :, column, :] * values[:, :, :, column : column + 1, :]
    return forces


def scatter_pairs(total_size, near_index, far_index, forces):
    return (
        jnp.zeros((total_size,), jnp.float32).at[near_index].add(forces).at[far_index].add(-forces)
    )


def ghost_shell(vector):
    return padded(vector, (("gx", 0), ("gy", 1), ("gz", 2)), 1)


def fold_back(summed):
    border = jnp.concatenate([summed[:, :, :1], summed[:, :, -1:]], axis=2)
    received = padded(border, (("gz", 2),), 1)
    interior = summed[:, :, 1:-1]
    interior = interior.at[:, :, :1].add(received[:, :, :1]).at[:, :, -1:].add(received[:, :, -1:])
    border = jnp.concatenate([interior[:, :1], interior[:, -1:]], axis=1)
    received = padded(border, (("gy", 1),), 1)
    interior = interior[:, 1:-1]
    interior = interior.at[:, :1].add(received[:, :1]).at[:, -1:].add(received[:, -1:])
    border = jnp.concatenate([interior[:1], interior[-1:]], axis=0)
    received = padded(border, (("gx", 0),), 1)
    interior = interior[1:-1]
    interior = interior.at[:1].add(received[:1]).at[-1:].add(received[-1:])
    return interior


def global_sums(values):
    return lax.psum(values, ("gx", "gy", "gz"))


def body(right_side, self_drag, pair_tensors, pair_first, pair_second, pair_count, particle_count):
    count_x, count_y, count_z, slot_count = pair_first.shape
    lane_count = right_side.shape[-1]
    along_x = jnp.arange(count_x, dtype=jnp.int32).reshape(-1, 1, 1, 1)
    along_y = jnp.arange(count_y, dtype=jnp.int32).reshape(1, -1, 1, 1)
    along_z = jnp.arange(count_z, dtype=jnp.int32).reshape(1, 1, -1, 1)
    offset = pair_second // lane_count
    far_slot = pair_second % lane_count
    step_x = offset // 9 - 1
    step_y = offset // 3 % 3 - 1
    step_z = offset % 3 - 1
    wide_y = count_y + 2
    wide_z = count_z + 2
    near_wide = ((along_x + 1) * wide_y + along_y + 1) * wide_z + along_z + 1 + 0 * pair_first
    far_wide = (
        ((along_x + 1 + step_x) * wide_y + along_y + 1 + step_y) * wide_z + along_z + 1 + step_z
    )
    near_wide_index = component_index(near_wide, pair_first, lane_count)
    far_wide_index = component_index(far_wide, far_slot, lane_count)
    slot_ids = jnp.arange(slot_count, dtype=jnp.int32)
    valid_pair = (slot_ids[None, None, None, :] < pair_count[:, :, :, None]).astype(jnp.float32)[
        :, :, :, None, :
    ]
    particle_slots = jnp.arange(lane_count, dtype=jnp.int32)
    live_mask = (particle_slots[None, None, None, :] < particle_count[:, :, :, None]).astype(
        jnp.float32
    )[:, :, :, None, :]
    residual = live_mask * right_side
    solution = jnp.zeros_like(residual)
    direction = residual
    norm_now = global_sums(jnp.stack([jnp.sum(residual * residual)]))[0]
    for iteration in range(ITERS):
        ghosted = ghost_shell(direction)
        flattened = ghosted.reshape(-1)
        difference = flattened[near_wide_index] - flattened[far_wide_index]
        forces = tensor_apply(pair_tensors, difference) * valid_pair
        wide_summed = scatter_pairs(ghosted.size, near_wide_index, far_wide_index, forces)
        summed = fold_back(wide_summed.reshape(ghosted.shape))
        applied = live_mask * (self_drag * direction + summed)
        step_size = norm_now / global_sums(jnp.stack([jnp.sum(direction * applied)]))[0]
        solution = solution + step_size * direction
        residual = residual - step_size * applied
        if iteration + 1 < ITERS:
            norm_next = global_sums(jnp.stack([jnp.sum(residual * residual)]))[0]
            direction = residual + norm_next / norm_now * direction
            norm_now = norm_next
    return (solution, residual)


def solution(mesh):
    return jax.shard_map(
        body,
        mesh=mesh,
        in_specs=(
            P("gx", "gy", "gz", None, None),
            P("gx", "gy", "gz", None, None),
            P("gx", "gy", "gz", None, None),
            P("gx", "gy", "gz", None),
            P("gx", "gy", "gz", None),
            P("gx", "gy", "gz"),
            P("gx", "gy", "gz"),
        ),
        out_specs=(P("gx", "gy", "gz", None, None), P("gx", "gy", "gz", None, None)),
        check_vma=False,
    )
```

profile of v0, /device:TPU:1, one launch (start us, length us, event | category | flops | bytes accessed | tf_op | source)
XLA Modules:
  0.0 519.1 jit_solution(15494404266402487193)
XLA Ops:
  1.3 10.5 %collective-permute-start.1 = (f32[1,1,1,6,128]{4,3,2,1,0:T(8,128)S(1)}, f32[1,1,1,6,128]{4,3,2,1,0:T(8,128)S(1)}, u32[]{:S(2)}, u32[]{:S(2)}) collective-permute-start(f32[1,1,1,6,128]{4,3,2,1,0:T(8,128)S(1)} %copy_multiply_fusion.2), channel_id=1, source_target_pairs={{48,0},{96,48},{144,96},{192,144},{240,192},{288,240},{336,288},{3... | collective-permute-start | bytes 9224 | tf_op jit(solution)/shard_map/ppermute | solution.py:17
  12.0 0.7 copy-done.4
  13.0 7.7 %collective-permute-start.3 = (f32[3,1,1,6,128]{4,3,2,1,0:T(8,128)S(1)}, f32[3,1,1,6,128]{4,3,2,1,0:T(8,128)S(1)}, u32[]{:S(2)}, u32[]{:S(2)}) collective-permute-start(f32[3,1,1,6,128]{4,3,2,1,0:T(8,128)S(1)} %pad_maximum_fusion.4), channel_id=1, source_target_pairs={{4,0},{8,4},{12,8},{16,12},{20,16},{24,20},{28,24},{32,28},{36,32}... | collective-permute-start | bytes 27656 | tf_op jit(solution)/shard_map/ppermute | solution.py:17
  20.7 1.9 collective-permute-start.2
  23.3 3.0 collective-permute-done.2
  26.4 4.4 collective-permute-start.5
  30.8 1.9 collective-permute-start.4
  32.7 4.0 collective-permute-done.4
  36.7 8.4 %gather_fusion.1 = f32[1536]{0:T(1024)S(1)} fusion(f32[20736]{0:T(1024)S(1)} %reshape.1702, s32[2048]{0:T(1024)S(1)} %pad_clamp_fusion), kind=kCustom, calls=%fused_computation.1 | custom fusion | bytes 18432 | tf_op jit(solution)/shard_map/gather | solution.py:99
  45.1 8.4 %gather_fusion = f32[1536]{0:T(1024)S(1)} fusion(f32[20736]{0:T(1024)S(1)} %reshape.1702, s32[2048]{0:T(1024)S(1)} %pad_clamp_fusion.1), kind=kCustom, calls=%fused_computation | custom fusion | bytes 18432 | tf_op jit(solution)/shard_map/gather | solution.py:99
  53.6 0.7 copy-done
  54.4 11.2 %scatter_custom_fusion = f32[20736]{0:T(1024)S(1)} fusion(s32[1536]{0:T(1024)S(1)} %reshape.1740, f32[1536]{0:T(1024)S(1)} %reshape.1742, f32[]{:T(128)} %constant.430.clone.1), kind=kCustom, calls=%fused_computation.12 | custom fusion | flops 1536 | bytes 82948 | tf_op jit(solution)/shard_map/scatter-add | solution.py:37
  65.6 8.8 %scatter_fusion = f32[20736]{0:T(1024)S(1)} fusion(f32[20736]{0:T(1024)S(1)} %scatter_custom_fusion, s32[1536]{0:T(1024)S(1)} %reshape.1716, f32[1536]{0:T(1024)S(1)} %reshape.1750), kind=kCustom, calls=%fused_computation.5 | custom fusion | flops 1536 | bytes 24576 | tf_op jit(solution)/shard_map/scatter-add | solution.py:37
  74.4 1.9 collective-permute-start.6
  76.3 4.6 collective-permute-start.7
  80.9 1.0 collective-permute-done.7
  82.0 1.9 collective-permute-start.8
  83.9 4.6 collective-permute-start.9
  88.5 0.8 collective-permute-done.9
  89.3 5.8 %collective-permute-start.10 = (f32[1,1,1,6,128]{4,3,2,1,0:T(8,128)S(1)}, f32[1,1,1,6,128]{4,3,2,1,0:T(8,128)S(1)}, u32[]{:S(2)}, u32[]{:S(2)}) collective-permute-start(f32[1,1,1,6,128]{4,3,2,1,0:T(8,128)S(1)} %get-tuple-element.267), channel_id=1, source_target_pairs={{0,48},{48,96},{96,144},{144,192},{192,240},{240,288},{288,336},{3... | collective-permute-start | bytes 9224 | tf_op jit(solution)/shard_map/ppermute | solution.py:16
  95.1 2.9 collective-permute-start.11
  98.1 0.6 collective-permute-done.10
  99.5 114.0 %all-reduce = (f32[1]{0:T(128)}, f32[1]{0:T(128)}) all-reduce(f32[1]{0:T(128)} %bitcast.1, f32[1]{0:T(128)} %bitcast.19), channel_id=1, replica_groups=mesh['gx'=16,'gy'=12,'gz'=4] {'gx','gy','gz'}, use_global_device_ids=true, to_apply=%region_1.2 | all-reduce | flops 2 | bytes 16 | tf_op jit(solution)/shard_map/psum | solution.py:62
  214.8 0.7 multiply_reduce_fusion.1
  215.5 103.7 %psum.30 = f32[1]{0:T(128)} all-reduce(f32[1]{0:T(128)} %bitcast.21), channel_id=1, replica_groups=mesh['gx'=16,'gy'=12,'gz'=4] {'gx','gy','gz'}, use_global_device_ids=true, to_apply=%region_7.8 | all-reduce | flops 1 | bytes 8 | tf_op jit(solution)/shard_map/psum | solution.py:62
  320.4 0.7 collective-permute-start.13
  321.1 1.1 collective-permute-start.12
  322.2 1.3 collective-permute-done.13
  323.5 3.7 collective-permute-start.15
  327.1 1.9 collective-permute-start.14
  329.1 3.7 collective-permute-done.14
  332.8 3.6 collective-permute-start.17
  336.4 1.9 collective-permute-start.16
  338.4 4.0 collective-permute-done.16
  342.4 8.4 %gather_fusion.3 = f32[1536]{0:T(1024)S(1)} fusion(f32[20736]{0:T(1024)S(1)} %reshape.1704, s32[2048]{0:T(1024)S(1)} %pad_clamp_fusion), kind=kCustom, calls=%fused_computation.3 | custom fusion | bytes 18432 | tf_op jit(solution)/shard_map/gather | solution.py:99
  350.8 8.4 %gather_fusion.2 = f32[1536]{0:T(1024)S(1)} fusion(f32[20736]{0:T(1024)S(1)} %reshape.1704, s32[2048]{0:T(1024)S(1)} %pad_clamp_fusion.1), kind=kCustom, calls=%fused_computation.2 | custom fusion | bytes 18432 | tf_op jit(solution)/shard_map/gather | solution.py:99
  359.3 11.2 %scatter_custom_fusion.2 = f32[20736]{0:T(1024)S(1)} fusion(s32[1536]{0:T(1024)S(1)} %reshape.1740, f32[1536]{0:T(1024)S(1)} %reshape.1758, f32[]{:T(128)} %constant.430.clone.1), kind=kCustom, calls=%fused_computation.10 | custom fusion | flops 1536 | bytes 82948 | tf_op jit(solution)/shard_map/scatter-add | solution.py:37
  370.5 8.8 %scatter_fusion.1 = f32[20736]{0:T(1024)S(1)} fusion(f32[20736]{0:T(1024)S(1)} %scatter_custom_fusion.2, s32[1536]{0:T(1024)S(1)} %reshape.1716, f32[1536]{0:T(1024)S(1)} %reshape.1766), kind=kCustom, calls=%fused_computation.7 | custom fusion | flops 1536 | bytes 24576 | tf_op jit(solution)/shard_map/scatter-add | solution.py:37
  379.4 1.9 collective-permute-start.18
  381.3 4.6 collective-permute-start.19
  385.9 1.0 collective-permute-done.19
  386.9 1.9 collective-permute-start.20
  388.9 4.6 collective-permute-start.21
  393.4 0.8 collective-permute-done.21
  394.3 6.9 %collective-permute-start.22 = (f32[1,1,1,6,128]{4,3,2,1,0:T(8,128)S(1)}, f32[1,1,1,6,128]{4,3,2,1,0:T(8,128)S(1)}, u32[]{:S(2)}, u32[]{:S(2)}) collective-permute-start(f32[1,1,1,6,128]{4,3,2,1,0:T(8,128)S(1)} %get-tuple-element.265), channel_id=1, source_target_pairs={{0,48},{48,96},{96,144},{144,192},{192,240},{240,288},{288,336},{3... | collective-permute-start | bytes 9224 | tf_op jit(solution)/shard_map/ppermute | solution.py:16
  401.3 0.6 collective-permute-done.22
  401.9 2.2 collective-permute-done.23
  404.8 111.9 %psum.31 = f32[1]{0:T(128)} all-reduce(f32[1]{0:T(128)} %bitcast.29), channel_id=1, replica_groups=mesh['gx'=16,'gy'=12,'gz'=4] {'gx','gy','gz'}, use_global_device_ids=true, to_apply=%region_11.12 | all-reduce | flops 1 | bytes 8 | tf_op jit(solution)/shard_map/psum | solution.py:62
  (72 shorter events, 3.6 us)
Async XLA Ops:
  0.6 0.7 copy-start.1
  1.3 10.6 %copy-start.3 = (s32[1,1,1,256]{3,2,1,0:T(1,128)S(1)}, s32[1,1,1,256]{3,2,1,0:T(1,128)}, u32[]{:S(2)}) copy-start(s32[1,1,1,256]{3,2,1,0:T(1,128)} %param.59) | copy-start | bytes 3076
  1.3 11.4 %collective-permute-start.1 = (f32[1,1,1,6,128]{4,3,2,1,0:T(8,128)S(1)}, f32[1,1,1,6,128]{4,3,2,1,0:T(8,128)S(1)}, u32[]{:S(2)}, u32[]{:S(2)}) collective-permute-start(f32[1,1,1,6,128]{4,3,2,1,0:T(8,128)S(1)} %copy_multiply_fusion.2), channel_id=1, source_target_pairs={{48,0},{96,48},{144,96},{192,144},{240,192},{288,240},{336,288},{3... | collective-permute-start | bytes 9224 | tf_op jit(solution)/shard_map/ppermute | solution.py:17
  11.9 1.2 collective-permute-start
  11.9 0.7 copy-start.4
  13.0 10.3 %collective-permute-start.3 = (f32[3,1,1,6,128]{4,3,2,1,0:T(8,128)S(1)}, f32[3,1,1,6,128]{4,3,2,1,0:T(8,128)S(1)}, u32[]{:S(2)}, u32[]{:S(2)}) collective-permute-start(f32[3,1,1,6,128]{4,3,2,1,0:T(8,128)S(1)} %pad_maximum_fusion.4), channel_id=1, source_target_pairs={{4,0},{8,4},{12,8},{16,12},{20,16},{24,20},{28,24},{32,28},{36,32}... | collective-permute-start | bytes 27656 | tf_op jit(solution)/shard_map/ppermute | solution.py:17
  20.7 5.7 %collective-permute-start.2 = (f32[3,1,1,6,128]{4,3,2,1,0:T(8,128)S(1)}, f32[3,1,1,6,128]{4,3,2,1,0:T(8,128)S(1)}, u32[]{:S(2)}, u32[]{:S(2)}) collective-permute-start(f32[3,1,1,6,128]{4,3,2,1,0:T(8,128)S(1)} %pad_maximum_fusion.4), channel_id=1, source_target_pairs={{0,4},{4,8},{8,12},{12,16},{16,20},{20,24},{24,28},{28,32},{32,36}... | collective-permute-start | bytes 27656 | tf_op jit(solution)/shard_map/ppermute | solution.py:16
  26.4 6.3 %collective-permute-start.5 = (f32[3,3,1,6,128]{4,3,2,1,0:T(8,128)S(1)}, f32[3,3,1,6,128]{4,3,2,1,0:T(8,128)S(1)}, u32[]{:S(2)}, u32[]{:S(2)}) collective-permute-start(f32[3,3,1,6,128]{4,3,2,1,0:T(8,128)S(1)} %pad_maximum_fusion.2), channel_id=1, source_target_pairs={{1,0},{2,1},{3,2},{0,3},{5,4},{6,5},{7,6},{4,7},{9,8},{10,9},{11,1... | collective-permute-start | bytes 82952 | tf_op jit(solution)/shard_map/ppermute | solution.py:17
  30.8 5.9 %collective-permute-start.4 = (f32[3,3,1,6,128]{4,3,2,1,0:T(8,128)S(1)}, f32[3,3,1,6,128]{4,3,2,1,0:T(8,128)S(1)}, u32[]{:S(2)}, u32[]{:S(2)}) collective-permute-start(f32[3,3,1,6,128]{4,3,2,1,0:T(8,128)S(1)} %pad_maximum_fusion.2), channel_id=1, source_target_pairs={{0,1},{1,2},{2,3},{3,0},{4,5},{5,6},{6,7},{7,4},{8,9},{9,10},{10,1... | collective-permute-start | bytes 82952 | tf_op jit(solution)/shard_map/ppermute | solution.py:16
  53.5 0.8 copy-start
  74.4 6.5 %collective-permute-start.6 = (f32[3,3,1,6,128]{4,3,2,1,0:T(8,128)S(1)}, f32[3,3,1,6,128]{4,3,2,1,0:T(8,128)S(1)}, u32[]{:S(2)}, u32[]{:S(2)}) collective-permute-start(f32[3,3,1,6,128]{4,3,2,1,0:T(8,128)S(1)} %get-tuple-element.259), channel_id=1, source_target_pairs={{0,1},{1,2},{2,3},{3,0},{4,5},{5,6},{6,7},{7,4},{8,9},{9,10},{10,1... | collective-permute-start | bytes 82952 | tf_op jit(solution)/shard_map/ppermute | solution.py:16
  76.3 5.6 %collective-permute-start.7 = (f32[3,3,1,6,128]{4,3,2,1,0:T(8,128)S(1)}, f32[3,3,1,6,128]{4,3,2,1,0:T(8,128)S(1)}, u32[]{:S(2)}, u32[]{:S(2)}) collective-permute-start(f32[3,3,1,6,128]{4,3,2,1,0:T(8,128)S(1)} %get-tuple-element.260), channel_id=1, source_target_pairs={{1,0},{2,1},{3,2},{0,3},{5,4},{6,5},{7,6},{4,7},{9,8},{10,9},{11,1... | collective-permute-start | bytes 82952 | tf_op jit(solution)/shard_map/ppermute | solution.py:17
  82.0 6.5 %collective-permute-start.8 = (f32[3,1,1,6,128]{4,3,2,1,0:T(8,128)S(1)}, f32[3,1,1,6,128]{4,3,2,1,0:T(8,128)S(1)}, u32[]{:S(2)}, u32[]{:S(2)}) collective-permute-start(f32[3,1,1,6,128]{4,3,2,1,0:T(8,128)S(1)} %get-tuple-element.263), channel_id=1, source_target_pairs={{0,4},{4,8},{8,12},{12,16},{16,20},{20,24},{24,28},{28,32},{32,36}... | collective-permute-start | bytes 27656 | tf_op jit(solution)/shard_map/ppermute | solution.py:16
  83.9 5.4 %collective-permute-start.9 = (f32[3,1,1,6,128]{4,3,2,1,0:T(8,128)S(1)}, f32[3,1,1,6,128]{4,3,2,1,0:T(8,128)S(1)}, u32[]{:S(2)}, u32[]{:S(2)}) collective-permute-start(f32[3,1,1,6,128]{4,3,2,1,0:T(8,128)S(1)} %get-tuple-element.264), channel_id=1, source_target_pairs={{4,0},{8,4},{12,8},{16,12},{20,16},{24,20},{28,24},{32,28},{36,32}... | collective-permute-start | bytes 27656 | tf_op jit(solution)/shard_map/ppermute | solution.py:17
  89.3 9.6 %copy-start.2 = (f32[1,1,1,6,128]{4,2,3,1,0:T(1,128)S(1)}, f32[1,1,1,6,128]{4,2,3,1,0:T(1,128)}, u32[]{:S(2)}) copy-start(f32[1,1,1,6,128]{4,2,3,1,0:T(1,128)} %param.56) | copy-start | bytes 9220
  89.3 9.4 %collective-permute-start.10 = (f32[1,1,1,6,128]{4,3,2,1,0:T(8,128)S(1)}, f32[1,1,1,6,128]{4,3,2,1,0:T(8,128)S(1)}, u32[]{:S(2)}, u32[]{:S(2)}) collective-permute-start(f32[1,1,1,6,128]{4,3,2,1,0:T(8,128)S(1)} %get-tuple-element.267), channel_id=1, source_target_pairs={{0,48},{48,96},{96,144},{144,192},{192,240},{240,288},{288,336},{3... | collective-permute-start | bytes 9224 | tf_op jit(solution)/shard_map/ppermute | solution.py:16
  95.1 3.8 collective-permute-start.11
  320.4 3.0 collective-permute-start.13
  321.1 2.4 collective-permute-start.12
  323.5 5.6 %collective-permute-start.15 = (f32[3,1,1,6,128]{4,3,2,1,0:T(8,128)S(1)}, f32[3,1,1,6,128]{4,3,2,1,0:T(8,128)S(1)}, u32[]{:S(2)}, u32[]{:S(2)}) collective-permute-start(f32[3,1,1,6,128]{4,3,2,1,0:T(8,128)S(1)} %pad_maximum_fusion.5), channel_id=1, source_target_pairs={{4,0},{8,4},{12,8},{16,12},{20,16},{24,20},{28,24},{32,28},{36,32}... | collective-permute-start | bytes 27656 | tf_op jit(solution)/shard_map/ppermute | solution.py:17
  327.1 5.7 %collective-permute-start.14 = (f32[3,1,1,6,128]{4,3,2,1,0:T(8,128)S(1)}, f32[3,1,1,6,128]{4,3,2,1,0:T(8,128)S(1)}, u32[]{:S(2)}, u32[]{:S(2)}) collective-permute-start(f32[3,1,1,6,128]{4,3,2,1,0:T(8,128)S(1)} %pad_maximum_fusion.5), channel_id=1, source_target_pairs={{0,4},{4,8},{8,12},{12,16},{16,20},{20,24},{24,28},{28,32},{32,36}... | collective-permute-start | bytes 27656 | tf_op jit(solution)/shard_map/ppermute | solution.py:16
  332.8 5.6 %collective-permute-start.17 = (f32[3,3,1,6,128]{4,3,2,1,0:T(8,128)S(1)}, f32[3,3,1,6,128]{4,3,2,1,0:T(8,128)S(1)}, u32[]{:S(2)}, u32[]{:S(2)}) collective-permute-start(f32[3,3,1,6,128]{4,3,2,1,0:T(8,128)S(1)} %pad_maximum_fusion.3), channel_id=1, source_target_pairs={{1,0},{2,1},{3,2},{0,3},{5,4},{6,5},{7,6},{4,7},{9,8},{10,9},{11,1... | collective-permute-start | bytes 82952 | tf_op jit(solution)/shard_map/ppermute | solution.py:17
  336.4 5.9 %collective-permute-start.16 = (f32[3,3,1,6,128]{4,3,2,1,0:T(8,128)S(1)}, f32[3,3,1,6,128]{4,3,2,1,0:T(8,128)S(1)}, u32[]{:S(2)}, u32[]{:S(2)}) collective-permute-start(f32[3,3,1,6,128]{4,3,2,1,0:T(8,128)S(1)} %pad_maximum_fusion.3), channel_id=1, source_target_pairs={{0,1},{1,2},{2,3},{3,0},{4,5},{5,6},{6,7},{7,4},{8,9},{9,10},{10,1... | collective-permute-start | bytes 82952 | tf_op jit(solution)/shard_map/ppermute | solution.py:16
  379.4 6.5 %collective-permute-start.18 = (f32[3,3,1,6,128]{4,3,2,1,0:T(8,128)S(1)}, f32[3,3,1,6,128]{4,3,2,1,0:T(8,128)S(1)}, u32[]{:S(2)}, u32[]{:S(2)}) collective-permute-start(f32[3,3,1,6,128]{4,3,2,1,0:T(8,128)S(1)} %get-tuple-element.257), channel_id=1, source_target_pairs={{0,1},{1,2},{2,3},{3,0},{4,5},{5,6},{6,7},{7,4},{8,9},{9,10},{10,1... | collective-permute-start | bytes 82952 | tf_op jit(solution)/shard_map/ppermute | solution.py:16
  381.3 5.6 %collective-permute-start.19 = (f32[3,3,1,6,128]{4,3,2,1,0:T(8,128)S(1)}, f32[3,3,1,6,128]{4,3,2,1,0:T(8,128)S(1)}, u32[]{:S(2)}, u32[]{:S(2)}) collective-permute-start(f32[3,3,1,6,128]{4,3,2,1,0:T(8,128)S(1)} %get-tuple-element.258), channel_id=1, source_target_pairs={{1,0},{2,1},{3,2},{0,3},{5,4},{6,5},{7,6},{4,7},{9,8},{10,9},{11,1... | collective-permute-start | bytes 82952 | tf_op jit(solution)/shard_map/ppermute | solution.py:17
  386.9 6.5 %collective-permute-start.20 = (f32[3,1,1,6,128]{4,3,2,1,0:T(8,128)S(1)}, f32[3,1,1,6,128]{4,3,2,1,0:T(8,128)S(1)}, u32[]{:S(2)}, u32[]{:S(2)}) collective-permute-start(f32[3,1,1,6,128]{4,3,2,1,0:T(8,128)S(1)} %get-tuple-element.261), channel_id=1, source_target_pairs={{0,4},{4,8},{8,12},{12,16},{16,20},{20,24},{24,28},{28,32},{32,36}... | collective-permute-start | bytes 27656 | tf_op jit(solution)/shard_map/ppermute | solution.py:16
  388.9 5.4 %collective-permute-start.21 = (f32[3,1,1,6,128]{4,3,2,1,0:T(8,128)S(1)}, f32[3,1,1,6,128]{4,3,2,1,0:T(8,128)S(1)}, u32[]{:S(2)}, u32[]{:S(2)}) collective-permute-start(f32[3,1,1,6,128]{4,3,2,1,0:T(8,128)S(1)} %get-tuple-element.262), channel_id=1, source_target_pairs={{4,0},{8,4},{12,8},{16,12},{20,16},{24,20},{28,24},{32,28},{36,32}... | collective-permute-start | bytes 27656 | tf_op jit(solution)/shard_map/ppermute | solution.py:17
  394.3 7.7 %collective-permute-start.22 = (f32[1,1,1,6,128]{4,3,2,1,0:T(8,128)S(1)}, f32[1,1,1,6,128]{4,3,2,1,0:T(8,128)S(1)}, u32[]{:S(2)}, u32[]{:S(2)}) collective-permute-start(f32[1,1,1,6,128]{4,3,2,1,0:T(8,128)S(1)} %get-tuple-element.265), channel_id=1, source_target_pairs={{0,48},{48,96},{96,144},{144,192},{192,240},{240,288},{288,336},{3... | collective-permute-start | bytes 9224 | tf_op jit(solution)/shard_map/ppermute | solution.py:16
  401.1 3.0 collective-permute-start.23
where the time goes:
time: 520 us; the launch traced here: 519 us
  blocking collectives  330 us (63%)
  starting transfers between devices  81.1 us (16%)
  other arithmetic  42.2 us (8%)
  local copies, waits for them, and re-layouts  36.3 us (7%)
  waiting for transfers between devices  23.6 us (5%)
  between operations  6.33 us (1%)
    psum x3, blocking collectives, global_sums(): return lax.psum(values, ('gx', 'gy', 'gz'))  330 us
    ppermute x12, starting transfers between devices, padded(): after = lax.ppermute(initial, axis, down)  52 us
    scatter-add x4, other arithmetic, scatter_pairs(): jnp.zeros((total_size,), jnp.float32).at[near_index].add(forces)  40 us
    gather x4, local copies, waits for them, and re-layouts, body(): difference = flattened[near_wide_index] - flattened[far_wide_index]  33.6 us
    ppermute x12, starting transfers between devices, padded(): before = lax.ppermute(last, axis, up)  29.1 us
    ppermute x12, waiting for transfers between devices, padded(): before = lax.ppermute(last, axis, up)  16.3 us
  transfers between devices with their start and end apart: 24, of which 14 were waited for; matrix products, arithmetic and copies ran while one was open for 0% of the time, Pallas kernels for 0%

commit v1 on v0

v1 whole, which is shorter than its diff:
```python
import functools

import jax
import jax.numpy as jnp
from jax import lax
from jax.experimental import pallas as pl
from jax.experimental.pallas import tpu as pltpu
from jax.sharding import PartitionSpec as P

AXES = ("gx", "gy", "gz")
LANES = 128
PAIRS = 256
OFFSETS = 27
CENTRE = 13
STEPS = [(o // 9 - 1, o // 3 % 3 - 1, o % 3 - 1) for o in range(OFFSETS)]
OTHERS = [o for o in range(OFFSETS) if o != CENTRE]


def phase_steps(sizes):
    nx, ny, nz = sizes
    return (
        [(k, 0, 0) for k in range(1, nx)],
        [(0, k, 0) for k in range(1, ny)],
        [(0, 0, k) for k in range(1, nz)],
    )


def kernel(
    sizes,
    rhs_ref,
    drag_ref,
    tensor_ref,
    first_ref,
    second_ref,
    pair_count_ref,
    particle_count_ref,
    sol_ref,
    res_ref,
    near_hot,
    far_hot,
    columns,
    vec_a,
    vec_b,
    halo_a,
    halo_b,
    masked,
    part_a,
    part_b,
    back_a,
    back_b,
    *rest,
):
    phases = phase_steps(sizes)
    count = len(phases)
    own = rest[: 2 * count]
    got = rest[2 * count : 4 * count]
    halo_send, halo_recv, back_send, back_recv = rest[4 * count : 4 * count + 4]
    sums_send, sums_recv = rest[4 * count + 4 : 4 * count + 6]
    me = tuple(lax.axis_index(axis) for axis in AXES)

    def device(step):
        return tuple(lax.rem(m + (s % n), n) for m, s, n in zip(me, step, sizes))

    def opposite(step):
        return tuple(-s for s in step)

    greeted = []
    for step in [STEPS[o] for o in OTHERS] + [s for phase in phases for s in phase]:
        wrapped = tuple(s % n for s, n in zip(step, sizes))
        if wrapped not in greeted:
            greeted.append(wrapped)
    barrier = pltpu.get_barrier_semaphore()
    for step in greeted:
        pl.semaphore_signal(
            barrier, inc=1, device_id=device(step), device_id_type=pl.DeviceIdType.MESH
        )

    def remote(src, dst, send, recv, step):
        return pltpu.make_async_remote_copy(
            src_ref=src,
            dst_ref=dst,
            send_sem=send,
            recv_sem=recv,
            device_id=device(step),
            device_id_type=pl.DeviceIdType.MESH,
        )

    def rows(o):
        return pl.ds(8 * o, 8)

    def halo_copy(turn, o):
        source, target = ((vec_a, halo_a), (vec_b, halo_b))[turn]
        return remote(
            source, target.at[rows(o)], halo_send.at[turn, o], halo_recv.at[turn, o],
            opposite(STEPS[o]),
        )

    def back_copy(turn, o):
        source, target = ((part_a, back_a), (part_b, back_b))[turn]
        return remote(
            source.at[rows(o)], target.at[rows(o)], back_send.at[turn, o], back_recv.at[turn, o],
            STEPS[o],
        )

    offsets_before = [sum(len(p) for p in phases[:i]) for i in range(count)]

    def sums_copy(turn, phase, k):
        at = offsets_before[phase] + k
        return remote(
            own[turn * count + phase],
            got[turn * count + phase].at[k],
            sums_send.at[turn, at],
            sums_recv.at[turn, at],
            phases[phase][k],
        )

    live = lax.broadcasted_iota(jnp.int32, (6, LANES), 1) < particle_count_ref[0]
    vec_a[...] = jnp.zeros_like(vec_a)
    vec_b[...] = jnp.zeros_like(vec_b)
    force = jnp.where(live, rhs_ref[...], 0.0)
    vec_a[0:6, :] = force
    halo_a[rows(CENTRE), :] = vec_a[...]
    drag = drag_ref[...]
    second = second_ref[...]
    offset = lax.shift_right_logical(second, 7)
    far_slot = lax.bitwise_and(second, 127)
    slots = lax.broadcasted_iota(jnp.int32, (LANES, PAIRS), 0)
    near_hot[...] = jnp.where(slots == first_ref[...], 1.0, 0.0).astype(jnp.bfloat16)
    far_hot[...] = jnp.where(slots == far_slot, 1.0, 0.0).astype(jnp.bfloat16)
    valid = lax.broadcasted_iota(jnp.int32, (1, PAIRS), 1) < pair_count_ref[0]
    columns[...] = jnp.zeros_like(columns)
    for r in range(6):
        for c in range(6):
            row = tensor_ref[6 * r + c : 6 * r + c + 1, :]
            columns[c, r : r + 1, :] = jnp.where(valid, row, 0.0)

    def pieces(x):
        high = x.astype(jnp.bfloat16)
        rest_1 = x - high.astype(jnp.float32)
        middle = rest_1.astype(jnp.bfloat16)
        low = (rest_1 - middle.astype(jnp.float32)).astype(jnp.bfloat16)
        return high, middle, low

    def gather(x, hot):
        dots = [jnp.dot(p, hot[...], preferred_element_type=jnp.float32) for p in pieces(x)]
        return dots[0] + dots[1] + dots[2]

    def scatter(x, hot):
        dots = [
            lax.dot_general(
                p, hot[...], (((1,), (1,)), ((), ())), preferred_element_type=jnp.float32
            )
            for p in pieces(x)
        ]
        return dots[0] + dots[1] + dots[2]

    def far_values(halo):
        wide = gather(halo[...], far_hot)
        total = jnp.zeros((8, PAIRS), jnp.float32)
        for o in range(OFFSETS):
            total = jnp.where(offset == o, wide[8 * o : 8 * o + 8, :], total)
        return total

    def pair_forces(difference):
        forces = columns[0] * difference[0:1, :]
        for c in range(1, 6):
            forces = forces + columns[c] * difference[c : c + 1, :]
        return forces

    def spread(forces, part):
        for o in range(OFFSETS):
            masked[rows(o), :] = jnp.where(offset == o, forces, 0.0)
        part[...] = scatter(masked[...], far_hot)

    def folded(near_sum, part, back):
        far_sum = part[rows(CENTRE), :]
        for o in OTHERS:
            far_sum = far_sum + back[rows(o), :]
        return (near_sum - far_sum)[0:6, :]

    lane_row = lax.broadcasted_iota(jnp.int32, (1, LANES), 1)

    def packed(values):
        total = jnp.zeros((1, LANES), jnp.float32)
        for at, value in enumerate(values):
            total = jnp.where(lane_row == at, value, total)
        return total

    def pick(row, at):
        return jnp.sum(jnp.where(lane_row == at, row, 0.0), axis=1, keepdims=True)

    def sums_start(turn, phase, value):
        own[turn * count + phase][...] = value
        for k in range(len(phases[phase])):
            sums_copy(turn, phase, k).start()

    def sums_finish(turn, phase, value):
        for k in range(len(phases[phase])):
            sums_copy(turn, phase, k).wait_recv()
        return value + jnp.sum(got[turn * count + phase][...], axis=0)

    def total_of(x):
        return jnp.sum(jnp.sum(x, axis=0, keepdims=True), axis=1, keepdims=True)

    def pair_total(x):
        return x[:, :LANES] + x[:, LANES:]

    near_a = gather(vec_a[...], near_hot)

    pl.semaphore_wait(barrier, len(greeted))

    for o in OTHERS:
        halo_copy(0, o).start()
    for o in OTHERS:
        halo_copy(0, o).wait_recv()
    diff_a = near_a - far_values(halo_a)
    forces_a = pair_forces(diff_a)
    sums_now = packed(
        [
            total_of(force * force),
            total_of(drag * force * force) + total_of(pair_total(diff_a * forces_a)),
        ]
    )
    sums_start(0, 0, sums_now)
    spread(forces_a, part_a)
    for o in OTHERS:
        back_copy(0, o).start()
    near_sum_a = scatter(forces_a, near_hot)
    for o in OTHERS:
        back_copy(0, o).wait_recv()
    image_a = jnp.where(live, drag * force + folded(near_sum_a, part_a, back_a), 0.0)
    vec_b[0:6, :] = image_a
    for o in OTHERS:
        halo_copy(1, o).start()
    halo_b[rows(CENTRE), :] = vec_b[...]
    near_b = gather(vec_b[...], near_hot)
    sums_now = sums_finish(0, 0, sums_now)
    sums_start(0, 1, sums_now)
    for o in OTHERS:
        halo_copy(1, o).wait_recv()
    diff_b = near_b - far_values(halo_b)
    sums_now = sums_finish(0, 1, sums_now)
    sums_start(0, 2, sums_now)
    sums_now = sums_finish(0, 2, sums_now)
    norm_a = pick(sums_now, 0)
    curve_a = pick(sums_now, 1)
    step_a = norm_a / curve_a

    residual = force - step_a * image_a
    diff_r = diff_a - step_a * diff_b
    forces_r = pair_forces(diff_r)
    dragged = drag * residual
    sums_now = packed(
        [
            total_of(residual * residual),
            total_of(dragged * residual) + total_of(pair_total(diff_r * forces_r)),
            total_of(residual * image_a)
            + total_of(dragged * force)
            + total_of(pair_total(diff_a * forces_r)),
        ]
    )
    sums_start(1, 0, sums_now)
    spread(forces_r, part_b)
    for o in OTHERS:
        back_copy(1, o).start()
    near_sum_r = scatter(forces_r, near_hot)
    sums_now = sums_finish(1, 0, sums_now)
    sums_start(1, 1, sums_now)
    for o in OTHERS:
        back_copy(1, o).wait_recv()
    image_r = jnp.where(live, dragged + folded(near_sum_r, part_b, back_b), 0.0)
    sums_now = sums_finish(1, 1, sums_now)
    sums_start(1, 2, sums_now)
    for turn in range(2):
        for o in OTHERS:
            halo_copy(turn, o).wait_send()
            back_copy(turn, o).wait_send()
    sums_now = sums_finish(1, 2, sums_now)
    norm_b = pick(sums_now, 0)
    ratio = norm_b / norm_a
    curve_b = pick(sums_now, 1) + ratio * (pick(sums_now, 2) + ratio * curve_a)
    step_b = norm_b / curve_b
    sol_ref[...] = step_a * force + step_b * (residual + ratio * force)
    res_ref[...] = residual - step_b * (image_r + ratio * image_a)
    for turn in range(2):
        for phase in range(count):
            for k in range(len(phases[phase])):
                sums_copy(turn, phase, k).wait_send()


def body(
    sizes,
    right_side,
    self_drag,
    pair_tensors,
    pair_first,
    pair_second,
    pair_count,
    particle_count,
):
    phases = phase_steps(sizes)
    steps = sum(len(phase) for phase in phases)
    vmem = pl.BlockSpec(memory_space=pltpu.VMEM)
    smem = pl.BlockSpec(memory_space=pltpu.SMEM)
    f32 = jnp.float32
    block = jax.ShapeDtypeStruct((6, LANES), f32)
    wide = pltpu.VMEM((8 * OFFSETS, LANES), f32)
    solution_value, residual_value = pl.pallas_call(
        functools.partial(kernel, sizes),
        out_shape=(block, block),
        in_specs=[vmem] * 5 + [smem] * 2,
        out_specs=(vmem, vmem),
        scratch_shapes=[
            pltpu.VMEM((LANES, PAIRS), jnp.bfloat16),
            pltpu.VMEM((LANES, PAIRS), jnp.bfloat16),
            pltpu.VMEM((6, 8, PAIRS), f32),
            pltpu.VMEM((8, LANES), f32),
            pltpu.VMEM((8, LANES), f32),
            wide,
            wide,
            pltpu.VMEM((8 * OFFSETS, PAIRS), f32),
            wide,
            wide,
            wide,
            wide,
        ]
        + [pltpu.VMEM((1, LANES), f32) for _ in range(2 * len(phases))]
        + [pltpu.VMEM((len(phase), 1, LANES), f32) for _ in range(2) for phase in phases]
        + [pltpu.SemaphoreType.DMA((2, OFFSETS))] * 4
        + [pltpu.SemaphoreType.DMA((2, steps))] * 2,
        compiler_params=pltpu.CompilerParams(collective_id=0, has_side_effects=True),
    )(
        right_side.reshape(6, LANES),
        self_drag.reshape(6, LANES),
        pair_tensors.reshape(36, PAIRS),
        pair_first.reshape(1, PAIRS),
        pair_second.reshape(1, PAIRS),
        pair_count.reshape(1),
        particle_count.reshape(1),
    )
    shape = right_side.shape
    return solution_value.reshape(shape), residual_value.reshape(shape)


def solution(mesh):
    sizes = tuple(mesh.shape[axis] for axis in AXES)
    return jax.shard_map(
        functools.partial(body, sizes),
        mesh=mesh,
        in_specs=(
            P("gx", "gy", "gz", None, None),
            P("gx", "gy", "gz", None, None),
            P("gx", "gy", "gz", None, None),
            P("gx", "gy", "gz", None),
            P("gx", "gy", "gz", None),
            P("gx", "gy", "gz"),
            P("gx", "gy", "gz"),
        ),
        out_specs=(P("gx", "gy", "gz", None, None), P("gx", "gy", "gz", None, None)),
        check_vma=False,
    )
```

time: 520 us -> 63.5 us (0.12)
  blocking collectives: 330 us -> 0 us
  starting transfers between devices: 81.1 us -> 0 us
  Pallas kernels: 0 us -> 56.5 us
  other arithmetic: 42.2 us -> 0 us
  local copies, waits for them, and re-layouts: 36.3 us -> 4.58 us
  waiting for transfers between devices: 23.6 us -> 0 us
    psum x3 -> x0, blocking collectives: 330 us -> none  [global_sums(): return lax.psum(values, ('gx', 'gy', 'gz'))]
    ppermute x24 -> x0, starting transfers between devices: 81.1 us -> none  [the longest x12 52 us: padded(): after = lax.ppermute(initial, axis, down)]
    pallas_call x0 -> x1, Pallas kernels: none -> 56.5 us  [body(): pl.pallas_call(functools.partial(kernel, sizes), out_shape=(block, block)...]
    scatter-add x4 -> x0, other arithmetic: 40 us -> none  [scatter_pairs(): jnp.zeros((total_size,), jnp.float32).at[near_index].add(forces)]
    gather x4 -> x0, local copies, waits for them, and re-layouts: 33.6 us -> none  [body(): difference = flattened[near_wide_index] - flattened[far_wide_index]]
    ppermute x24 -> x0, waiting for transfers between devices: 23.6 us -> none  [the longest x12 16.3 us: padded(): before = lax.ppermute(last, axis, up)]
  transfers between devices with their start and end apart: 24 -> 0, of which waited for: 14 -> 0; matrix products, arithmetic and copies ran while one was open for 0% -> 0% of each run, Pallas kernels for 0% -> 0%
where the time goes in v1:
time: 63.5 us; the launch traced here: 63.1 us
  Pallas kernels  56.5 us (89%)
  local copies, waits for them, and re-layouts  4.58 us (7%)
  between operations  1.98 us (3%)
    pallas_call x1, Pallas kernels, body(): pl.pallas_call(functools.partial(kernel, sizes), out_shape=(block, block)...  56.5 us
    unnamed x12, local copies, waits for them, and re-layouts  4.58 us

profile of v1, /device:TPU:1, one launch (start us, length us, event | category | flops | bytes accessed | tf_op | source)
XLA Modules:
  0.0 63.1 jit_solution(10973050610582977711)
XLA Ops:
  1.3 0.0 copy-start.3
  1.9 0.0 copy-start.2
  2.0 0.0 copy-done.3
  2.0 0.7 %copy-done.2 = f32[1,1,1,6,128]{4,2,3,1,0:T(1,128)S(1)} copy-done((f32[1,1,1,6,128]{4,2,3,1,0:T(1,128)S(1)}, f32[1,1,1,6,128]{4,2,3,1,0:T(1,128)}, u32[]{:S(2)}) %copy-start.2) | copy-done | bytes 3096
  2.6 0.6 copy_bitcast_fusion.1
  3.2 1.4 %copy.17 = f32[1,1,1,36,256]{4,3,2,1,0:T(8,128)} copy(f32[1,1,1,36,256]{4,2,3,1,0:T(1,128)} %param.9) | data formatting | bytes 73728
  4.6 56.5 %shard_map.86 = (f32[6,128]{1,0:T(8,128)}, f32[6,128]{1,0:T(8,128)}) custom-call(f32[6,128]{1,0:T(8,128)} %get-tuple-element.9.rhs_ref, f32[6,128]{1,0:T(8,128)} %get-tuple-element.8.drag_ref, f32[36,256]{1,0:T(8,128)} %bitcast.15, s32[1,256]{1,0:T(1,128)} %bitcast.18, s32[1,256]{1,0:T(1,128)} %bitcast.19, s32[1]{0:T(128)} %bitcast.13.pair_count_ref, ...), custom_call_target="tpu_custom_call" | custom-call | tf_op jit(solution)/shard_map/pallas_call | solution.py:308
  61.1 0.0 copy-start.1
  61.1 0.7 %copy-done.1 = f32[6,128]{1,0:T(8,128)S(1)} copy-done((f32[6,128]{1,0:T(8,128)S(1)}, f32[6,128]{1,0:T(8,128)}, u32[]{:S(2)}) %copy-start.1) | copy-done | bytes 3096
  61.8 0.0 copy-start
  61.8 0.6 copy.9
  62.4 0.1 copy-done
  62.5 0.6 copy.10
Async XLA Ops:
  1.3 0.7 %copy-start.3 = (f32[1,1,1,6,128]{4,2,3,1,0:T(1,128)S(1)}, f32[1,1,1,6,128]{4,2,3,1,0:T(1,128)}, u32[]{:S(2)}) copy-start(f32[1,1,1,6,128]{4,2,3,1,0:T(1,128)} %param.7) | copy-start | bytes 9220
  1.9 0.7 %copy-start.2 = (f32[1,1,1,6,128]{4,2,3,1,0:T(1,128)S(1)}, f32[1,1,1,6,128]{4,2,3,1,0:T(1,128)}, u32[]{:S(2)}) copy-start(f32[1,1,1,6,128]{4,2,3,1,0:T(1,128)} %param.8) | copy-start | bytes 9220
  61.1 0.7 %copy-start.1 = (f32[6,128]{1,0:T(8,128)S(1)}, f32[6,128]{1,0:T(8,128)}, u32[]{:S(2)}) copy-start(f32[6,128]{1,0:T(8,128)} %get-tuple-element.4) | copy-start | bytes 9220
  61.8 0.7 %copy-start = (f32[6,128]{1,0:T(8,128)S(1)}, f32[6,128]{1,0:T(8,128)}, u32[]{:S(2)}) copy-start(f32[6,128]{1,0:T(8,128)} %get-tuple-element.5) | copy-start | bytes 9220

commit v2 on v1

v2 whole, which is shorter than its diff:
```python
import functools

import jax
import jax.numpy as jnp
from jax import lax
from jax.experimental import pallas as pl
from jax.experimental.pallas import tpu as pltpu
from jax.sharding import PartitionSpec as P

AXES = ("gx", "gy", "gz")
LANES = 128
PAIRS = 256
OFFSETS = 27
CENTRE = 13
STEPS = [(o // 9 - 1, o // 3 % 3 - 1, o % 3 - 1) for o in range(OFFSETS)]
OTHERS = sorted(
    (o for o in range(OFFSETS) if o != CENTRE), key=lambda o: -sum(abs(s) for s in STEPS[o])
)

SLOT = [o - (o > CENTRE) if o != CENTRE else OFFSETS - 1 for o in range(OFFSETS)]


def far_first(steps, lengths):
    def hops(step):
        return sum(min(s % n, -s % n) for s, n in zip(step, lengths))

    return sorted(steps, key=hops, reverse=True)


def phase_steps(sizes):
    nx, ny, nz = sizes
    lengths = (nx // 2, 2, ny, nz)
    return (
        far_first([(0, c, k, 0) for k in range(ny) for c in range(2)], lengths)[:-1],
        far_first([(j, 0, 0, k) for k in range(nz) for j in range(nx // 2)], lengths)[:-1],
    )


def kernel(
    sizes,
    rhs_ref,
    drag_ref,
    tensor_ref,
    first_ref,
    second_ref,
    pair_count_ref,
    particle_count_ref,
    out_ref,
    near_hot,
    far_hot,
    columns,
    vec_a,
    vec_b,
    halo_a,
    halo_b,
    masked,
    part_a,
    part_b,
    back_a,
    back_b,
    rhs_v,
    drag_v,
    first_v,
    second_v,
    tensor_v,
    pair_count_s,
    particle_count_s,
    drag_rows,
    load_sem,
    *rest,
):
    phases = phase_steps(sizes)
    count = len(phases)
    own = rest[: 2 * count]
    got = rest[2 * count : 4 * count]
    halo_send, halo_recv, back_send, back_recv = rest[4 * count : 4 * count + 4]
    sums_send, sums_recv = rest[4 * count + 4 : 4 * count + 6]
    loaded = (rhs_v, drag_v, first_v, second_v, tensor_v, pair_count_s, particle_count_s)
    given = (
        rhs_ref, drag_ref, first_ref, second_ref, tensor_ref, pair_count_ref, particle_count_ref,
    )
    loads = [
        pltpu.make_async_copy(src, dst, load_sem.at[at])
        for at, (src, dst) in enumerate(zip(given, loaded))
    ]
    for load in loads:
        load.start()
    me = tuple(lax.axis_index(axis) for axis in AXES)

    known = {}

    def shifted(axis, by):
        by = by % sizes[axis]
        if by == 0:
            return me[axis]
        if (axis, by) not in known:
            known[axis, by] = lax.rem(me[axis] + by, sizes[axis])
        return known[axis, by]

    def device(step):
        if len(step) == 3:
            return tuple(shifted(axis, by) for axis, by in enumerate(step))
        row, side, y, z = step
        if ("x", row, side) not in known:
            across = shifted(0, 2 * row)
            if side:
                across = across + 1 - 2 * lax.rem(across, 2)
            known["x", row, side] = across
        return known["x", row, side], shifted(1, y), shifted(2, z)

    def opposite(step):
        return tuple(-s for s in step)

    near_steps = [tuple(s % n for s, n in zip(STEPS[o], sizes)) for o in OTHERS]
    greeted = [s for phase in phases for s in phase]
    greeted = [s for s in greeted if s[1] or (2 * s[0], s[2], s[3]) not in near_steps]
    greeted = greeted + near_steps
    barrier = pltpu.get_barrier_semaphore()
    for step in greeted:
        pl.semaphore_signal(
            barrier, inc=1, device_id=device(step), device_id_type=pl.DeviceIdType.MESH
        )

    def remote(src, dst, send, recv, step):
        return pltpu.make_async_remote_copy(
            src_ref=src,
            dst_ref=dst,
            send_sem=send,
            recv_sem=recv,
            device_id=device(step),
            device_id_type=pl.DeviceIdType.MESH,
        )

    def rows(o):
        return pl.ds(8 * SLOT[o], 8)

    def wait_all(buffer, sem):
        pltpu.make_async_copy(buffer, buffer, sem).wait()

    arriving = pl.ds(0, 8 * (OFFSETS - 1))

    def halo_copy(turn, o):
        source, target = ((vec_a, halo_a), (vec_b, halo_b))[turn]
        return remote(
            source, target.at[rows(o)], halo_send.at[turn], halo_recv.at[turn],
            opposite(STEPS[o]),
        )

    def back_copy(turn, o):
        source, target = ((part_a, back_a), (part_b, back_b))[turn]
        return remote(
            source.at[rows(o)], target.at[rows(o)], back_send.at[turn], back_recv.at[turn],
            STEPS[o],
        )

    def sums_copy(turn, phase, k):
        at = turn * count + phase
        return remote(
            own[turn * count + phase],
            got[turn * count + phase].at[k],
            sums_send.at[at],
            sums_recv.at[at],
            phases[phase][k],
        )

    loads[5].wait()
    loads[6].wait()
    live = lax.broadcasted_iota(jnp.int32, (6, LANES), 1) < particle_count_s[0, 0, 0]
    vec_a[...] = jnp.zeros_like(vec_a)
    loads[0].wait()
    for r in range(6):
        vec_a[r : r + 1, :] = jnp.where(live[0:1], rhs_v[r], 0.0)
    pl.semaphore_wait(barrier, len(greeted))
    for o in OTHERS:
        halo_copy(0, o).start()
    vec_b[...] = jnp.zeros_like(vec_b)
    columns[...] = jnp.zeros_like(columns)
    loads[1].wait()
    for r in range(6):
        drag_rows[r : r + 1, :] = drag_v[r]
    force = vec_a[0:6, :]
    halo_a[rows(CENTRE), :] = vec_a[...]
    drag = drag_rows[...]
    loads[2].wait()
    loads[3].wait()
    second = second_v[...]
    offset = lax.shift_right_logical(second, 7)
    far_slot = lax.bitwise_and(second, 127)
    slots = lax.broadcasted_iota(jnp.int32, (LANES, PAIRS), 0)
    near_hot[...] = jnp.where(slots == first_v[...], 1.0, 0.0).astype(jnp.bfloat16)
    far_hot[...] = jnp.where(slots == far_slot, 1.0, 0.0).astype(jnp.bfloat16)
    valid = lax.broadcasted_iota(jnp.int32, (1, PAIRS), 1) < pair_count_s[0, 0, 0]
    loads[4].wait()
    for r in range(6):
        for c in range(6):
            columns[c, r : r + 1, :] = jnp.where(valid, tensor_v[6 * r + c], 0.0)

    def pieces(x):
        high = x.astype(jnp.bfloat16)
        rest_1 = x - high.astype(jnp.float32)
        middle = rest_1.astype(jnp.bfloat16)
        low = (rest_1 - middle.astype(jnp.float32)).astype(jnp.bfloat16)
        return high, middle, low

    def stacked(x):
        return jnp.concatenate(pieces(x), axis=0)

    def unstacked(wide):
        height = wide.shape[0] // 3
        return wide[:height] + wide[height : 2 * height] + wide[2 * height :]

    def gather(x, hot):
        return unstacked(jnp.dot(stacked(x), hot[...], preferred_element_type=jnp.float32))

    def scatter(x, hot):
        return unstacked(
            lax.dot_general(
                stacked(x),
                hot[...],
                (((1,), (1,)), ((), ())),
                preferred_element_type=jnp.float32,
            )
        )

    def far_values(halo):
        wide = gather(halo[...], far_hot)
        total = jnp.zeros((8, PAIRS), jnp.float32)
        for o in range(OFFSETS):
            total = jnp.where(offset == o, wide[8 * SLOT[o] : 8 * SLOT[o] + 8, :], total)
        return total

    def pair_forces(difference):
        forces = columns[0] * difference[0:1, :]
        for c in range(1, 6):
            forces = forces + columns[c] * difference[c : c + 1, :]
        return forces

    def spread(forces, part):
        for o in range(OFFSETS):
            masked[rows(o), :] = jnp.where(offset == o, forces, 0.0)
        part[...] = scatter(masked[...], far_hot)

    def folded(near_sum, part, back):
        far_sum = part[rows(CENTRE), :]
        for o in OTHERS:
            far_sum = far_sum + back[rows(o), :]
        return (near_sum - far_sum)[0:6, :]

    lane_row = lax.broadcasted_iota(jnp.int32, (1, LANES), 1)

    def packed(values):
        total = jnp.zeros((1, LANES), jnp.float32)
        for at, value in enumerate(values):
            total = jnp.where(lane_row == at, value, total)
        return total

    def pick(row, at):
        return jnp.sum(jnp.where(lane_row == at, row, 0.0), axis=1, keepdims=True)

    def sums_start(turn, phase, value):
        own[turn * count + phase][...] = value
        for k in range(len(phases[phase])):
            sums_copy(turn, phase, k).start()

    def sums_finish(turn, phase, value):
        wait_all(got[turn * count + phase], sums_recv.at[turn * count + phase])
        return value + jnp.sum(got[turn * count + phase][...], axis=0)

    def total_of(x):
        return jnp.sum(jnp.sum(x, axis=0, keepdims=True), axis=1, keepdims=True)

    def pair_total(x):
        return x[:, :LANES] + x[:, LANES:]

    near_a = gather(vec_a[...], near_hot)

    wait_all(halo_a.at[arriving], halo_recv.at[0])
    diff_a = near_a - far_values(halo_a)
    forces_a = pair_forces(diff_a)
    spread(forces_a, part_a)
    for o in OTHERS:
        back_copy(0, o).start()
    sums_now = packed(
        [
            total_of(force * force),
            total_of(drag * force * force) + total_of(pair_total(diff_a * forces_a)),
        ]
    )
    sums_start(0, 0, sums_now)
    near_sum_a = scatter(forces_a, near_hot)
    wait_all(back_a.at[arriving], back_recv.at[0])
    image_a = jnp.where(live, drag * force + folded(near_sum_a, part_a, back_a), 0.0)
    vec_b[0:6, :] = image_a
    for o in OTHERS:
        halo_copy(1, o).start()
    halo_b[rows(CENTRE), :] = vec_b[...]
    sums_now = sums_finish(0, 0, sums_now)
    sums_start(0, 1, sums_now)
    near_b = gather(vec_b[...], near_hot)
    wait_all(halo_b.at[arriving], halo_recv.at[1])
    diff_b = near_b - far_values(halo_b)
    sums_now = sums_finish(0, 1, sums_now)
    norm_a = pick(sums_now, 0)
    curve_a = pick(sums_now, 1)
    step_a = norm_a / curve_a

    residual = force - step_a * image_a
    diff_r = diff_a - step_a * diff_b
    forces_r = pair_forces(diff_r)
    dragged = drag * residual
    sums_now = packed(
        [
            total_of(residual * residual),
            total_of(dragged * residual) + total_of(pair_total(diff_r * forces_r)),
            total_of(residual * image_a)
            + total_of(dragged * force)
            + total_of(pair_total(diff_a * forces_r)),
        ]
    )
    sums_start(1, 0, sums_now)
    spread(forces_r, part_b)
    for o in OTHERS:
        back_copy(1, o).start()
    near_sum_r = scatter(forces_r, near_hot)
    sums_now = sums_finish(1, 0, sums_now)
    sums_start(1, 1, sums_now)
    wait_all(back_b.at[arriving], back_recv.at[1])
    image_r = jnp.where(live, dragged + folded(near_sum_r, part_b, back_b), 0.0)
    for turn, (halo, back) in enumerate(((halo_a, back_a), (halo_b, back_b))):
        wait_all(halo.at[arriving], halo_send.at[turn])
        wait_all(back.at[arriving], back_send.at[turn])
    for at in range(2 * count - 1):
        wait_all(got[at], sums_send.at[at])
    sums_now = sums_finish(1, 1, sums_now)
    norm_b = pick(sums_now, 0)
    ratio = norm_b / norm_a
    curve_b = pick(sums_now, 1) + ratio * (pick(sums_now, 2) + ratio * curve_a)
    step_b = norm_b / curve_b
    sol = step_a * force + step_b * (residual + ratio * force)
    res = residual - step_b * (image_r + ratio * image_a)
    for r in range(6):
        out_ref[0, r] = sol[r : r + 1, :]
        out_ref[1, r] = res[r : r + 1, :]
    wait_all(got[2 * count - 1], sums_send.at[2 * count - 1])


def body(
    sizes,
    right_side,
    self_drag,
    pair_tensors,
    pair_first,
    pair_second,
    pair_count,
    particle_count,
):
    phases = phase_steps(sizes)
    vmem = pl.BlockSpec(memory_space=pltpu.VMEM)
    f32 = jnp.float32
    both = jax.ShapeDtypeStruct((2, 6, 1, LANES), f32)
    wide = pltpu.VMEM((8 * OFFSETS, LANES), f32)
    both_values = pl.pallas_call(
        functools.partial(kernel, sizes),
        out_shape=both,
        in_specs=[pl.BlockSpec(memory_space=pltpu.HBM)] * 7,
        out_specs=vmem,
        scratch_shapes=[
            pltpu.VMEM((LANES, PAIRS), jnp.bfloat16),
            pltpu.VMEM((LANES, PAIRS), jnp.bfloat16),
            pltpu.VMEM((6, 8, PAIRS), f32),
            pltpu.VMEM((8, LANES), f32),
            pltpu.VMEM((8, LANES), f32),
            wide,
            wide,
            pltpu.VMEM((8 * OFFSETS, PAIRS), f32),
            wide,
            wide,
            wide,
            wide,
            pltpu.VMEM((6, 1, LANES), f32),
            pltpu.VMEM((6, 1, LANES), f32),
            pltpu.VMEM((1, PAIRS), jnp.int32),
            pltpu.VMEM((1, PAIRS), jnp.int32),
            pltpu.VMEM((36, 1, PAIRS), f32),
            pltpu.SMEM((1, 1, 1), jnp.int32),
            pltpu.SMEM((1, 1, 1), jnp.int32),
            pltpu.VMEM((6, LANES), f32),
            pltpu.SemaphoreType.DMA((7,)),
        ]
        + [pltpu.VMEM((1, LANES), f32) for _ in range(2 * len(phases))]
        + [pltpu.VMEM((len(phase), 1, LANES), f32) for _ in range(2) for phase in phases]
        + [pltpu.SemaphoreType.DMA((2,))] * 4
        + [pltpu.SemaphoreType.DMA((2 * len(phases),))] * 2,
        compiler_params=pltpu.CompilerParams(collective_id=0, has_side_effects=True),
    )(
        right_side.reshape(6, 1, LANES),
        self_drag.reshape(6, 1, LANES),
        pair_tensors.reshape(36, 1, PAIRS),
        pair_first.reshape(1, PAIRS),
        pair_second.reshape(1, PAIRS),
        pair_count,
        particle_count,
    )
    shape = right_side.shape
    return both_values[0].reshape(shape), both_values[1].reshape(shape)


def solution(mesh):
    sizes = tuple(mesh.shape[axis] for axis in AXES)
    return jax.shard_map(
        functools.partial(body, sizes),
        mesh=mesh,
        in_specs=(
            P("gx", "gy", "gz", None, None),
            P("gx", "gy", "gz", None, None),
            P("gx", "gy", "gz", None, None),
            P("gx", "gy", "gz", None),
            P("gx", "gy", "gz", None),
            P("gx", "gy", "gz"),
            P("gx", "gy", "gz"),
        ),
        out_specs=(P("gx", "gy", "gz", None, None), P("gx", "gy", "gz", None, None)),
        check_vma=False,
    )
```

time: 63.5 us -> 52.8 us (0.83)
  Pallas kernels: 56.5 us -> 49.4 us
  local copies, waits for them, and re-layouts: 4.58 us -> 1.26 us
    pallas_call x1, Pallas kernels: 56.5 us -> 49.4 us  [body(): pl.pallas_call(functools.partial(kernel, sizes), out_shape=both, in_specs...]
    unnamed x12 -> x1, local copies, waits for them, and re-layouts: 4.58 us -> 1.26 us
where the time goes in v2:
time: 52.8 us; the launch traced here: 52.6 us
  Pallas kernels  49.4 us (94%)
  between operations  1.93 us (4%)
  local copies, waits for them, and re-layouts  1.26 us (2%)
    pallas_call x1, Pallas kernels, body(): pl.pallas_call(functools.partial(kernel, sizes), out_shape=both, in_specs...  49.4 us
    unnamed x1, local copies, waits for them, and re-layouts  1.26 us

profile of v2, /device:TPU:1, one launch (start us, length us, event | category | flops | bytes accessed | tf_op | source)
XLA Modules:
  0.0 52.6 jit_solution(16552222515302943747)
XLA Ops:
  1.9 49.4 %shard_map.86 = f32[2,6,1,128]{3,2,1,0:T(1,128)} custom-call(f32[6,1,128]{2,1,0:T(1,128)} %bitcast.14, f32[6,1,128]{2,1,0:T(1,128)} %bitcast.15, f32[36,1,256]{2,1,0:T(1,128)} %bitcast.13, s32[1,256]{1,0:T(1,128)} %bitcast.16, s32[1,256]{1,0:T(1,128)} %bitcast.17, s32[1,1,1]{2,1,0:T(1,128)S(6)} %copy.11.pair_count_ref, s32[1,1,1]{2,1,0:T(1,128)S(6)} %copy.12.particle_count_ref), custom_call_target="tpu_custom_call" | custom-call | tf_op jit(solution)/shard_map/pallas_call | solution.py:362
  51.4 1.3 %slice_bitcast_fusion = (f32[1,1,1,6,128]{4,2,3,1,0:T(1,128)}, f32[1,1,1,6,128]{4,2,3,1,0:T(1,128)}) fusion(f32[2,6,1,128]{3,2,1,0:T(1,128)} %shard_map.86), kind=kLoop, calls=%fused_computation | loop fusion | bytes 12288

commit v3 on v2

--- a/solution.py
+++ b/solution.py
@@ -114,7 +114,7 @@
     near_steps = [tuple(s % n for s, n in zip(STEPS[o], sizes)) for o in OTHERS]
     greeted = [s for phase in phases for s in phase]
     greeted = [s for s in greeted if s[1] or (2 * s[0], s[2], s[3]) not in near_steps]
-    greeted = greeted + near_steps
+    greeted = near_steps + greeted
     barrier = pltpu.get_barrier_semaphore()
     for step in greeted:
         pl.semaphore_signal(
@@ -277,9 +277,6 @@
     wait_all(halo_a.at[arriving], halo_recv.at[0])
     diff_a = near_a - far_values(halo_a)
     forces_a = pair_forces(diff_a)
-    spread(forces_a, part_a)
-    for o in OTHERS:
-        back_copy(0, o).start()
     sums_now = packed(
         [
             total_of(force * force),
@@ -287,6 +284,9 @@
         ]
     )
     sums_start(0, 0, sums_now)
+    spread(forces_a, part_a)
+    for o in OTHERS:
+        back_copy(0, o).start()
     near_sum_a = scatter(forces_a, near_hot)
     wait_all(back_a.at[arriving], back_recv.at[0])
     image_a = jnp.where(live, drag * force + folded(near_sum_a, part_a, back_a), 0.0)
@@ -299,7 +299,10 @@
     near_b = gather(vec_b[...], near_hot)
     wait_all(halo_b.at[arriving], halo_recv.at[1])
     diff_b = near_b - far_values(halo_b)
-    sums_now = sums_finish(0, 1, sums_now)
+    for phase in range(1, count - 1):
+        sums_now = sums_finish(0, phase, sums_now)
+        sums_start(0, phase + 1, sums_now)
+    sums_now = sums_finish(0, count - 1, sums_now)
     norm_a = pick(sums_now, 0)
     curve_a = pick(sums_now, 1)
     step_a = norm_a / curve_a
@@ -326,12 +329,15 @@
     sums_start(1, 1, sums_now)
     wait_all(back_b.at[arriving], back_recv.at[1])
     image_r = jnp.where(live, dragged + folded(near_sum_r, part_b, back_b), 0.0)
+    for phase in range(1, count - 1):
+        sums_now = sums_finish(1, phase, sums_now)
+        sums_start(1, phase + 1, sums_now)
     for turn, (halo, back) in enumerate(((halo_a, back_a), (halo_b, back_b))):
         wait_all(halo.at[arriving], halo_send.at[turn])
         wait_all(back.at[arriving], back_send.at[turn])
     for at in range(2 * count - 1):
         wait_all(got[at], sums_send.at[at])
-    sums_now = sums_finish(1, 1, sums_now)
+    sums_now = sums_finish(1, count - 1, sums_now)
     norm_b = pick(sums_now, 0)
     ratio = norm_b / norm_a
     curve_b = pick(sums_now, 1) + ratio * (pick(sums_now, 2) + ratio * curve_a)

time: 52.8 us -> 52.4 us (level)
  no operation moved by 1% of the time
where the time goes in v3:
time: 52.4 us; the launch traced here: 52.2 us
  Pallas kernels  49 us (94%)
  between operations  1.93 us (4%)
  local copies, waits for them, and re-layouts  1.26 us (2%)
    pallas_call x1, Pallas kernels, body(): pl.pallas_call(functools.partial(kernel, sizes), out_shape=both, in_specs...  49 us
    unnamed x1, local copies, waits for them, and re-layouts  1.26 us

profile of v3, /device:TPU:1, one launch (start us, length us, event | category | flops | bytes accessed | tf_op | source)
XLA Modules:
  0.0 52.2 jit_solution(6022586567729783593)
XLA Ops:
  1.9 49.0 %shard_map.86 = f32[2,6,1,128]{3,2,1,0:T(1,128)} custom-call(f32[6,1,128]{2,1,0:T(1,128)} %bitcast.14, f32[6,1,128]{2,1,0:T(1,128)} %bitcast.15, f32[36,1,256]{2,1,0:T(1,128)} %bitcast.13, s32[1,256]{1,0:T(1,128)} %bitcast.16, s32[1,256]{1,0:T(1,128)} %bitcast.17, s32[1,1,1]{2,1,0:T(1,128)S(6)} %copy.11.pair_count_ref, s32[1,1,1]{2,1,0:T(1,128)S(6)} %copy.12.particle_count_ref), custom_call_target="tpu_custom_call" | custom-call | tf_op jit(solution)/shard_map/pallas_call | solution.py:368
  50.9 1.3 %slice_bitcast_fusion = (f32[1,1,1,6,128]{4,2,3,1,0:T(1,128)}, f32[1,1,1,6,128]{4,2,3,1,0:T(1,128)}) fusion(f32[2,6,1,128]{3,2,1,0:T(1,128)} %shard_map.86), kind=kLoop, calls=%fused_computation | loop fusion | bytes 12288

commit v4 on v3

--- a/solution.py
+++ b/solution.py
@@ -134,22 +134,25 @@
     def rows(o):
         return pl.ds(8 * SLOT[o], 8)
 
+    def six(o):
+        return pl.ds(8 * SLOT[o], 6)
+
     def wait_all(buffer, sem):
         pltpu.make_async_copy(buffer, buffer, sem).wait()
 
-    arriving = pl.ds(0, 8 * (OFFSETS - 1))
+    arriving = pl.ds(0, 6 * (OFFSETS - 1))
 
     def halo_copy(turn, o):
         source, target = ((vec_a, halo_a), (vec_b, halo_b))[turn]
         return remote(
-            source, target.at[rows(o)], halo_send.at[turn], halo_recv.at[turn],
+            source.at[pl.ds(0, 6)], target.at[six(o)], halo_send.at[turn], halo_recv.at[turn],
             opposite(STEPS[o]),
         )
 
     def back_copy(turn, o):
         source, target = ((part_a, back_a), (part_b, back_b))[turn]
         return remote(
-            source.at[rows(o)], target.at[rows(o)], back_send.at[turn], back_recv.at[turn],
+            source.at[six(o)], target.at[six(o)], back_send.at[turn], back_recv.at[turn],
             STEPS[o],
         )
 
@@ -270,7 +273,7 @@
         return jnp.sum(jnp.sum(x, axis=0, keepdims=True), axis=1, keepdims=True)
 
     def pair_total(x):
-        return x[:, :LANES] + x[:, LANES:]
+        return x[0:6, :LANES] + x[0:6, LANES:]
 
     near_a = gather(vec_a[...], near_hot)
 

time: 52.4 us -> 52.3 us (level)
  no operation moved by 1% of the time
where the time goes in v4:
time: 52.3 us; the launch traced here: 52.1 us
  Pallas kernels  48.9 us (93%)
  between operations  1.93 us (4%)
  local copies, waits for them, and re-layouts  1.26 us (2%)
    pallas_call x1, Pallas kernels, body(): pl.pallas_call(functools.partial(kernel, sizes), out_shape=both, in_specs...  48.9 us
    unnamed x1, local copies, waits for them, and re-layouts  1.26 us

profile of v4, /device:TPU:1, one launch (start us, length us, event | category | flops | bytes accessed | tf_op | source)
XLA Modules:
  0.0 52.1 jit_solution(2690469492100352080)
XLA Ops:
  1.9 48.9 %shard_map.86 = f32[2,6,1,128]{3,2,1,0:T(1,128)} custom-call(f32[6,1,128]{2,1,0:T(1,128)} %bitcast.14, f32[6,1,128]{2,1,0:T(1,128)} %bitcast.15, f32[36,1,256]{2,1,0:T(1,128)} %bitcast.13, s32[1,256]{1,0:T(1,128)} %bitcast.16, s32[1,256]{1,0:T(1,128)} %bitcast.17, s32[1,1,1]{2,1,0:T(1,128)S(6)} %copy.11.pair_count_ref, s32[1,1,1]{2,1,0:T(1,128)S(6)} %copy.12.particle_count_ref), custom_call_target="tpu_custom_call" | custom-call | tf_op jit(solution)/shard_map/pallas_call | solution.py:371
  50.8 1.3 %slice_bitcast_fusion = (f32[1,1,1,6,128]{4,2,3,1,0:T(1,128)}, f32[1,1,1,6,128]{4,2,3,1,0:T(1,128)}) fusion(f32[2,6,1,128]{3,2,1,0:T(1,128)} %shard_map.86), kind=kLoop, calls=%fused_computation | loop fusion | bytes 12288
